TPU v7x, 256 devices: a whole 4x4x8 slice. The times are simulated.
256 devices in a mesh: bulk: 16 (over z_lo, x), tp: 16 (over z_hi, y, core).
Axes of the slice: x: 4, y: 4, z: 8 (z_hi: 2, z_lo: 4; z = z_hi * 4 + z_lo), core: 2. Of those that a mesh axis runs over, the one named last changes fastest.
Arguments:
- queries: bfloat16 [16384, 8192], P('bulk', 'tp'), may hold values from -40 to 40, as said below
- comp_keys: bfloat16 [16384, 1024], P(('bulk', 'tp')), may hold values from -8 to 8
- comp_values: bfloat16 [16384, 1024], P(('bulk', 'tp')), may hold values from -6 to 6
- prefix_keys: bfloat16 [16, 2048, 1024], P('bulk', 'tp'), may hold values from -10 to 10
- prefix_values: bfloat16 [16, 2048, 1024], P('bulk', 'tp'), may hold values from -6 to 6
- lengths: int32 [16, 16], P('bulk'), may hold values from 1 to 64, as said below
- routing: int32 [16, 64], P('bulk'), may hold values from 0 to 15, as said below
- residual: bfloat16 [16384, 8192], P('bulk', 'tp'), may hold values from -6 to 6
- out_weight: bfloat16 [8192, 8192], P('tp'), may hold values from -0.09375 to 0.09375
Outputs:
- mixed: bfloat16 [8192, 8192], P('bulk', 'tp')
Inputs may be any that keep to these rules, and one draw needn't show every extreme that they name: queries are of order one except on some rows of the hidden draw. `lengths`: for every prompt, the sum over its completions of ceil(length / 8) is at most 64, and it equals 64 for some prompt in every draw. `routing`: in every row, each index of bulk appears exactly 4 times.
All inputs are finite; a program needn't handle non-finite values.
Results may differ from a plain program's by a relative error of at most 0.009.
Values may be sent and summed in bfloat16 or wider, within the bound.
A program may use at most 128 MiB of HBM per device.

v0:
```python
import math

import jax
import jax.numpy as jnp
import numpy as np
from jax import lax
from jax.sharding import PartitionSpec as P

HEADS = 64
KVH = 8
HD = 128
CMAX = 64
GROUP = 16
BLK = 8
SLOTS = 64


def side_by_side(arrays, axis, split_dim, concat_dim, along):
    widths = [a.shape[along] for a in arrays]
    both = jnp.concatenate(arrays, axis=along)
    whole = lax.all_to_all(both, axis, split_axis=split_dim, concat_axis=concat_dim, tiled=True)
    return tuple(jnp.split(whole, [sum(widths[:k]) for k in range(1, len(widths))], axis=along))


def tables(lens_row, route_row, per_pair):
    per_comp = CMAX // BLK
    counts = (lens_row + BLK - 1) // BLK
    inner = jnp.arange(per_comp, dtype=jnp.int32)
    live_flags = (inner[None, :] < counts[:, None]).reshape(-1).astype(jnp.int32)
    live_rank = jnp.cumsum(live_flags) - 1
    block_total = live_flags.shape[0]
    slot_order = jnp.arange(SLOTS, dtype=jnp.int32)
    rank_hits = (live_rank[:, None] == slot_order[None, :]) & (live_flags[:, None] == 1)
    block_ids = jnp.arange(block_total, dtype=jnp.int32)
    block_of = jnp.sum(jnp.where(rank_hits, block_ids[:, None], 0), axis=0)
    slot_used = jnp.any(rank_hits, axis=0)
    same_dest = route_row[:, None] == route_row[None, :]
    earlier = slot_order[None, :] < slot_order[:, None]
    slot_place = route_row * per_pair + jnp.sum(same_dest & earlier, axis=1)
    place_hits = slot_place[None, :] == slot_order[:, None]
    block_for = jnp.sum(jnp.where(place_hits, block_of[None, :], 0), axis=1)
    live_for = jnp.any(place_hits & slot_used[None, :], axis=1)
    return (block_for, live_for)


def attend(query_blk, key_own, value_own, key_pre, value_pre, lens_blk):
    inv_root = 1.0 / math.sqrt(query_blk.shape[-1])
    score_pre = (
        jnp.einsum("bckqh,pkh->bckqp", query_blk, key_pre, preferred_element_type=jnp.float32)
        * inv_root
    )
    score_own = (
        jnp.einsum("bckqh,bekh->bckqe", query_blk, key_own, preferred_element_type=jnp.float32)
        * inv_root
    )
    positions = jnp.arange(query_blk.shape[1], dtype=jnp.int32)
    causal = positions[None, :] <= positions[:, None]
    score_own = jnp.where(causal[None, :, None, None, :], score_own, jnp.float32(-1e30))
    top_score = jnp.maximum(jnp.max(score_pre, axis=-1), jnp.max(score_own, axis=-1))
    expo_pre = jnp.exp(score_pre - top_score[..., None])
    expo_own = jnp.exp(score_own - top_score[..., None])
    total = jnp.sum(expo_pre, axis=-1) + jnp.sum(expo_own, axis=-1)
    summed = jnp.einsum(
        "bckqp,pkh->bckqh",
        expo_pre.astype(jnp.bfloat16),
        value_pre,
        preferred_element_type=jnp.float32,
    )
    summed = summed + jnp.einsum(
        "bckqe,bekh->bckqh",
        expo_own.astype(jnp.bfloat16),
        value_own,
        preferred_element_type=jnp.float32,
    )
    result = summed / total[..., None]
    valid = positions[None, :] < lens_blk[:, None]
    result = jnp.where(valid[:, :, None, None, None], result, jnp.float32(0.0))
    return result.astype(jnp.bfloat16)


def pack_rows(row_data, block_for, live_for):
    blocks = row_data.reshape(-1, BLK, row_data.shape[-1])
    picked = jnp.take(blocks, block_for, axis=0)
    picked = jnp.where(live_for[:, None, None], picked, jnp.zeros((), row_data.dtype))
    return picked.reshape(-1, row_data.shape[-1])


def project(context, out_weight):
    return (
        lax.psum_scatter(
            lax.dot_general(
                out_weight, context, (((0,), (1,)), ((), ())), preferred_element_type=jnp.float32
            ).astype(jnp.bfloat16),
            "tp",
            scatter_dimension=0,
            tiled=True,
        )
        .astype(jnp.float32)
        .T
    )


def local(
    queries,
    comp_keys,
    comp_values,
    prefix_keys,
    prefix_values,
    lengths,
    routing,
    residual,
    out_weight,
):
    tp_count = lax.axis_size("tp")
    bulk_count = lax.axis_size("bulk")
    group_size = HEADS // KVH
    heads_loc = HEADS // tp_count
    kv_local = max(1, heads_loc // group_size)
    per_kv = heads_loc // kv_local
    head_table = np.array(
        [
            target * heads_loc // group_size + inner
            for target in range(tp_count)
            for inner in range(kv_local)
        ],
        dtype=np.int32,
    )

    def spread(cache):
        picked = cache.reshape(-1, KVH, HD)[:, head_table, :]
        return picked.reshape(-1, tp_count * kv_local * HD)

    near_keys, near_values, own_keys, own_values = (
        lax.all_to_all(spread(prefix_keys), "tp", split_axis=1, concat_axis=0, tiled=True),
        lax.all_to_all(spread(prefix_values), "tp", split_axis=1, concat_axis=0, tiled=True),
        lax.all_to_all(spread(comp_keys), "tp", split_axis=1, concat_axis=0, tiled=True),
        lax.all_to_all(spread(comp_values), "tp", split_axis=1, concat_axis=0, tiled=True),
    )
    per_block = max(1, min(GROUP, 512 // (CMAX * heads_loc)))
    block_count = GROUP // per_block
    lens_row = lengths.reshape(GROUP)
    query_blocks = queries.reshape(block_count, per_block, CMAX, kv_local, per_kv, HD)
    key_blocks = own_keys.reshape(block_count, per_block, CMAX, kv_local, HD)
    value_blocks = own_values.reshape(block_count, per_block, CMAX, kv_local, HD)
    lens_blocks = lens_row.reshape(block_count, per_block)
    key_pre = near_keys.reshape(-1, kv_local, HD)
    value_pre = near_values.reshape(-1, kv_local, HD)

    def one_block(bundle):
        return attend(bundle[0], bundle[1], bundle[2], key_pre, value_pre, bundle[3])

    context = lax.map(one_block, (query_blocks, key_blocks, value_blocks, lens_blocks))
    context = context.reshape(GROUP * CMAX, heads_loc * HD)
    row_ids = jnp.arange(GROUP * CMAX, dtype=jnp.int32)
    row_valid = row_ids % CMAX < lens_row[row_ids // CMAX]
    block_for, live_for = tables(lens_row, routing.reshape(SLOTS), SLOTS // bulk_count)
    resid_kept = jnp.where(row_valid[:, None], residual, jnp.zeros((), jnp.bfloat16))
    context_sent, resid_sent = side_by_side(
        (pack_rows(context, block_for, live_for), pack_rows(resid_kept, block_for, live_for)),
        "bulk",
        0,
        0,
        1,
    )
    summed = project(context_sent, out_weight)
    mixed = (resid_sent.astype(jnp.float32) + summed).astype(jnp.bfloat16)
    return mixed


def solution(mesh):
    return jax.shard_map(
        local,
        mesh=mesh,
        in_specs=(
            P("bulk", "tp"),
            P(("bulk", "tp"), None),
            P(("bulk", "tp"), None),
            P("bulk", "tp", None),
            P("bulk", "tp", None),
            P("bulk", None),
            P("bulk", None),
            P("bulk", "tp"),
            P("tp", None),
        ),
        out_specs=P("bulk", "tp"),
        check_vma=False,
    )
```

profile of v0, /device:TPU:2, one launch (start us, length us, event | category | flops | bytes accessed | tf_op | source)
XLA Modules:
  0.0 338.1 jit_solution(560144184113292791)
XLA Ops:
  7.6 1.3 gather_fusion.1
  8.9 11.3 %all-to-all-start.1 = ((bf16[64,16,128]{2,0,1:T(8,128)(2,1)}), bf16[64,16,128]{2,0,1:T(8,128)(2,1)S(1)}, u32[]{:S(2)}, u32[]{:S(2)}) async-start(bf16[64,16,128]{2,0,1:T(8,128)(2,1)} %bitcast.37), calls=%async_computation.1 | async-start | bytes 524288 | tf_op jit(solution)/shard_map/all_to_all | solution.py:136
  20.2 0.9 copy_bitcast_fusion.3
  21.1 1.3 gather_fusion.3
  22.4 9.8 %all-to-all-done.1 = bf16[64,16,128]{2,0,1:T(8,128)(2,1)S(1)} async-done(((bf16[64,16,128]{2,0,1:T(8,128)(2,1)}), bf16[64,16,128]{2,0,1:T(8,128)(2,1)S(1)}, u32[]{:S(2)}, u32[]{:S(2)}) %all-to-all-start.1) | async-done | bytes 262176 | tf_op jit(solution)/shard_map/all_to_all | solution.py:136
  32.3 0.7 copy-done.2
  33.0 3.5 %all-to-all-start.3 = ((bf16[64,16,128]{2,0,1:T(8,128)(2,1)}), bf16[64,16,128]{2,0,1:T(8,128)(2,1)S(1)}, u32[]{:S(2)}, u32[]{:S(2)}) async-start(bf16[64,16,128]{2,0,1:T(8,128)(2,1)} %bitcast.45), calls=%async_computation.3 | async-start | bytes 524288 | tf_op jit(solution)/shard_map/all_to_all | solution.py:137
  37.5 1.1 copy.37
  38.8 1.4 gather_fusion
  40.5 1.4 gather_fusion.2
  42.3 6.3 %all-to-all-done.3 = bf16[64,16,128]{2,0,1:T(8,128)(2,1)S(1)} async-done(((bf16[64,16,128]{2,0,1:T(8,128)(2,1)}), bf16[64,16,128]{2,0,1:T(8,128)(2,1)S(1)}, u32[]{:S(2)}, u32[]{:S(2)}) %all-to-all-start.3) | async-done | bytes 262176 | tf_op jit(solution)/shard_map/all_to_all | solution.py:137
  48.6 4.1 %all-to-all-start = ((bf16[128,16,128]{2,0,1:T(8,128)(2,1)}), bf16[128,16,128]{2,0,1:T(8,128)(2,1)S(1)}, u32[]{:S(2)}, u32[]{:S(2)}) async-start(bf16[128,16,128]{2,0,1:T(8,128)(2,1)} %bitcast.34), calls=%async_computation | async-start | bytes 1048576 | tf_op jit(solution)/shard_map/all_to_all | solution.py:134
  53.8 13.7 %all-to-all-done = bf16[128,16,128]{2,0,1:T(8,128)(2,1)S(1)} async-done(((bf16[128,16,128]{2,0,1:T(8,128)(2,1)}), bf16[128,16,128]{2,0,1:T(8,128)(2,1)S(1)}, u32[]{:S(2)}, u32[]{:S(2)}) %all-to-all-start) | async-done | bytes 524320 | tf_op jit(solution)/shard_map/all_to_all | solution.py:134
  67.5 7.0 %all-to-all-start.2 = ((bf16[128,16,128]{2,0,1:T(8,128)(2,1)}), bf16[128,16,128]{2,0,1:T(8,128)(2,1)}, u32[]{:S(2)}, u32[]{:S(2)}) async-start(bf16[128,16,128]{2,0,1:T(8,128)(2,1)} %bitcast.42), calls=%async_computation.2 | async-start | bytes 1048576 | tf_op jit(solution)/shard_map/all_to_all | solution.py:135
  74.5 4.3 %compare_select_fusion.1 = s32[1024,1]{0,1:T(1,128)S(1)} fusion(s32[]{:T(128)} %bitcast.59, s32[]{:T(128)} %bitcast.60, s32[]{:T(128)} %bitcast.61, s32[]{:T(128)} %bitcast.62, s32[]{:T(128)} %bitcast.63, s32[]{:T(128)} %bitcast.65, s32[]{:T(128)} %bitcast.64), kind=kLoop, calls=%fused_computation.80 | loop fusion | flops 23552 | bytes 4124 | tf_op jit(solution)/shard_map/gather | solution.py:155
  80.7 5.6 %fusion.53 = pred[1024]{0:T(1024)(128)(4,1)S(1)} fusion(pred[1024]{0:T(1024)(128)(4,1)S(1)} %compare_reduce_fusion, pred[1024]{0:T(1024)(128)(4,1)S(1)} %compare_reduce_fusion.1, pred[1024]{0:T(1024)(128)(4,1)S(1)} %compare_reduce_fusion.2, pred[1024]{0:T(1024)(128)(4,1)S(1)} %compare_reduce_fusion.3, pred[1024]{0:T(1024)(128)(4,1)S(1)} %compare_reduce_fusion.4, ...), kind=kLoop, calls=%fused_computation.93 | loop fusion | flops 16384 | bytes 14372 | tf_op jit(solution)/shard_map/lt | solution.py:155
  86.3 1.4 select_bitcast_fusion
  88.5 0.8 fusion.49
  89.9 47.2 %while.10 = (s32[]{:T(128)}, bf16[8,2,64,1,4,128]{5,4,2,1,0,3:T(4,128)(2,1)}, s32[8,2]{1,0:T(8,128)S(1)}, bf16[8,2,64,1,4,128]{5,4,2,1,0,3:T(4,128)(2,1)S(1)}, b...) while((s32[]{:T(128)}, ...), condition=%wide.region_9.10_spmd, body=%wide.region_4.9_spmd.sunk | while | flops 562531456 | bytes 15704465 | solution.py:152
  90.1 1.0 fusion.76
  91.1 0.8 bitcast_reduce_fusion.2
  92.2 0.8 fusion.77
  93.1 2.0 fusion.80
  95.1 0.7 copy_dynamic-update-slice_fusion.2
  96.0 1.0 fusion.76
  97.0 0.8 bitcast_reduce_fusion.2
  98.1 0.8 fusion.77
  99.0 2.0 fusion.80
  101.0 0.8 copy_dynamic-update-slice_fusion.2
  101.9 1.0 fusion.76
  102.9 0.8 bitcast_reduce_fusion.2
  104.0 0.8 fusion.77
  104.9 2.0 fusion.80
  106.9 0.8 copy_dynamic-update-slice_fusion.2
  107.8 1.0 fusion.76
  108.8 0.8 bitcast_reduce_fusion.2
  109.9 0.8 fusion.77
  110.8 2.0 fusion.80
  112.8 0.8 copy_dynamic-update-slice_fusion.2
  113.7 1.0 fusion.76
  114.7 0.8 bitcast_reduce_fusion.2
  115.8 0.8 fusion.77
  116.7 2.0 fusion.80
  118.7 0.8 copy_dynamic-update-slice_fusion.2
  119.6 1.0 fusion.76
  120.6 0.8 bitcast_reduce_fusion.2
  121.7 0.8 fusion.77
  122.6 2.0 fusion.80
  124.6 0.7 copy_dynamic-update-slice_fusion.2
  125.5 1.0 fusion.76
  126.5 0.8 bitcast_reduce_fusion.2
  127.6 0.8 fusion.77
  128.5 2.0 fusion.80
  130.5 0.8 copy_dynamic-update-slice_fusion.2
  131.4 1.0 fusion.76
  132.4 0.8 bitcast_reduce_fusion.2
  133.5 0.8 fusion.77
  134.4 2.0 fusion.80
  136.4 0.8 copy_dynamic-update-slice_fusion.2
  137.2 1.5 reshape_reshape.7
  139.6 36.6 %all_to_all.61 = bf16[16,32,1024]{2,1,0:T(8,128)(2,1)S(1)} all-to-all(bf16[16,32,1024]{2,1,0:T(8,128)(2,1)S(1)} %pad_maximum_fusion), channel_id=1, replica_groups=mesh['bulk'=16,'tp'=16] {'bulk'}, dimensions={0} | all-to-all | bytes 2097152 | tf_op jit(solution)/shard_map/all_to_all | solution.py:21
  176.2 10.1 %fusion.44 = bf16[8192,512]{0,1:T(8,128)(2,1)} fusion(bf16[512,8192]{1,0:T(8,128)(2,1)} %param.26, bf16[512,1024]{1,0:T(8,128)(2,1)S(1)} %bitcast.225), kind=kOutput, calls=%fused_computation.48 | convolution fusion | flops 4299161600 | bytes 17301504 | tf_op jit(solution)/shard_map/dot_general | solution.py:91
  186.2 143.0 %reduce-scatter.2.cloned.1.call-done = bf16[512,512]{0,1:T(8,128)(2,1)} async-done(((bf16[8192,512]{0,1:T(8,128)(2,1)}), bf16[512,512]{0,1:T(8,128)(2,1)}) %reduce-scatter.2.cloned.1.call-update) | async-done | bytes 524304 | tf_op jit(solution)/shard_map/reduce_scatter | solution.py:90
  329.2 2.0 fusion.45
  (120 shorter events, 11.8 us)
Async XLA Ops:
  6.5 1.0 copy-start
  6.5 46.5 %copy-start.4 = (s32[1,16]{1,0:T(1,128)S(1)}, s32[1,16]{1,0:T(1,128)}, u32[]{:S(2)}) copy-start(s32[1,16]{1,0:T(1,128)} %param.23) | copy-start | bytes 196
  6.5 33.6 %copy-start.3 = (bf16[1,128,1024]{2,1,0:T(8,128)(2,1)S(1)}, bf16[1,128,1024]{2,1,0:T(8,128)(2,1)}, u32[]{:S(2)}) copy-start(bf16[1,128,1024]{2,1,0:T(8,128)(2,1)} %param.22) | copy-start | bytes 786436
  6.5 46.2 %copy-start.5 = (s32[1,64]{1,0:T(1,128)S(1)}, s32[1,64]{1,0:T(1,128)}, u32[]{:S(2)}) copy-start(s32[1,64]{1,0:T(1,128)} %param.24) | copy-start | bytes 772
  8.9 71.2 %copy-start.1 = (bf16[1024,512]{1,0:T(8,128)(2,1)S(1)}, bf16[1024,512]{1,0:T(8,128)(2,1)}, u32[]{:S(2)}) copy-start(bf16[1024,512]{1,0:T(8,128)(2,1)} %param.18) | copy-start | bytes 3145732
  8.9 23.4 %all-to-all-start.1 = ((bf16[64,16,128]{2,0,1:T(8,128)(2,1)}), bf16[64,16,128]{2,0,1:T(8,128)(2,1)S(1)}, u32[]{:S(2)}, u32[]{:S(2)}) async-start(bf16[64,16,128]{2,0,1:T(8,128)(2,1)} %bitcast.37), calls=%async_computation.1 | async-start | bytes 524288 | tf_op jit(solution)/shard_map/all_to_all | solution.py:136
  32.3 0.7 copy-start.2
  33.0 15.6 %all-to-all-start.3 = ((bf16[64,16,128]{2,0,1:T(8,128)(2,1)}), bf16[64,16,128]{2,0,1:T(8,128)(2,1)S(1)}, u32[]{:S(2)}, u32[]{:S(2)}) async-start(bf16[64,16,128]{2,0,1:T(8,128)(2,1)} %bitcast.45), calls=%async_computation.3 | async-start | bytes 524288 | tf_op jit(solution)/shard_map/all_to_all | solution.py:137
  48.6 18.9 %all-to-all-start = ((bf16[128,16,128]{2,0,1:T(8,128)(2,1)}), bf16[128,16,128]{2,0,1:T(8,128)(2,1)S(1)}, u32[]{:S(2)}, u32[]{:S(2)}) async-start(bf16[128,16,128]{2,0,1:T(8,128)(2,1)} %bitcast.34), calls=%async_computation | async-start | bytes 1048576 | tf_op jit(solution)/shard_map/all_to_all | solution.py:134
  52.9 27.2 %copy-start.7 = (s32[64]{0:T(128)}, s32[64]{0:T(128)S(1)}, u32[]{:S(2)}) copy-start(s32[64]{0:T(128)S(1)} %fusion.57) | copy-start | bytes 772
  53.0 21.5 %copy-start.6 = (s32[64]{0:T(128)}, s32[64]{0:T(128)S(1)}, u32[]{:S(2)}) copy-start(s32[64]{0:T(128)S(1)} %select_reduce_fusion) | copy-start | bytes 772
  67.5 22.4 %all-to-all-start.2 = ((bf16[128,16,128]{2,0,1:T(8,128)(2,1)}), bf16[128,16,128]{2,0,1:T(8,128)(2,1)}, u32[]{:S(2)}, u32[]{:S(2)}) async-start(bf16[128,16,128]{2,0,1:T(8,128)(2,1)} %bitcast.42), calls=%async_computation.2 | async-start | bytes 1048576 | tf_op jit(solution)/shard_map/all_to_all | solution.py:135
  74.4 254.8 %reduce-scatter.2.cloned.1.call-start = ((), (), s32[]{:S(2)}) async-start(), calls=%async_computation.6 | async-start | bytes 8912896 | tf_op jit(solution)/shard_map/reduce_scatter | solution.py:90
Sparse Core Ops, SparseCore 0:
  186.4 142.8 reduce-scatter.1
where the time goes:
time: 340 us; the launch traced here: 338 us
  waiting for transfers between devices  173 us (51%)
  matrix products  42.3 us (12%)
  blocking collectives  36.6 us (11%)
  other arithmetic  26.4 us (8%)
  starting transfers between devices  25.9 us (8%)
  local copies, waits for them, and re-layouts  20 us (6%)
  between operations  13.6 us (4%)
    reduce_scatter x1, waiting for transfers between devices, project(): lax.psum_scatter(lax.dot_general(out_weight, context, (((0,), (1,)), ((),...  143 us
    all_to_all x1, blocking collectives, side_by_side(): lax.all_to_all(both, axis, split_axis=split_dim, concat_axis=concat_dim,...  36.6 us
    dot_general x8, matrix products, attend(): jnp.einsum('bckqp,pkh->bckqh', expo_pre.astype(jnp.bfloat16), value_pre,...  15.8 us
    all_to_all x1, waiting for transfers between devices, local(): lax.all_to_all(spread(prefix_keys), 'tp', split_axis=1, concat_axis=0, ti...  13.7 us
    all_to_all x1, starting transfers between devices, local(): lax.all_to_all(spread(comp_keys), 'tp', split_axis=1, concat_axis=0, tile...  11.3 us
    dot_general x1, matrix products, project(): lax.dot_general(out_weight, context, (((0,), (1,)), ((), ())), preferred_...  10.1 us
    all_to_all x1, waiting for transfers between devices, local(): lax.all_to_all(spread(comp_keys), 'tp', split_axis=1, concat_axis=0, tile...  9.84 us
    dot_general x8, matrix products, attend(): jnp.einsum('bckqh,bekh->bckqe', query_blk, key_own, preferred_element_typ...  8.21 us
  transfers between devices with their start and end apart: 5, of which 4 were waited for; matrix products, arithmetic and copies ran while one was open for 7% of the time, Pallas kernels for 0%

commit v1 on v0

v1 whole, which is shorter than its diff:
```python
import math

import jax
import jax.numpy as jnp
from jax import lax
from jax.experimental import pallas as pl
from jax.experimental.pallas import tpu as pltpu
from jax.sharding import PartitionSpec as P

HD = 128
BLK = 8
NX, NY, NZL, NZH, NC = 4, 4, 4, 2, 2
NK = NX
CR = 128
LH = 4
FE = 512
SCALE = math.log2(math.e) / math.sqrt(HD)
F32, BF16 = jnp.float32, jnp.bfloat16
MESH = pl.DeviceIdType.MESH
NT = (((1,), (1,)), ((), ()))


def position():
    b, t = lax.axis_index("bulk"), lax.axis_index("tp")
    x, zl = lax.rem(b, NX), lax.div(b, NX)
    c, y, zh = lax.rem(t, NC), lax.rem(lax.div(t, NC), NY), lax.div(t, NC * NY)
    return x, zl, c, y, zh


def tables_kernel(lens, route, blk, nval, count):
    x, zl, _, _, _ = position()

    def clear(p, carry):
        blk[p] = 0
        nval[p] = 0
        return carry

    lax.fori_loop(0, 64, clear, 0)

    def clear_count(d, carry):
        count[d] = 0
        return carry

    lax.fori_loop(0, 16, clear_count, 0)

    def completion(i, j):
        size = lens[0, i]
        blocks = lax.div(size + BLK - 1, BLK)

        def block(n, carry):
            d = route[0, j + n]
            seen = count[d]
            count[d] = seen + 1
            k = lax.rem(lax.rem(d, NX) - x + 2 * NX - 1, NX)
            dz = lax.rem(lax.div(d, NX) - zl + NZL, NZL)
            p = (k * NZL + dz) * 4 + seen
            blk[p] = i * 8 + n
            nval[p] = jnp.minimum(size - n * BLK, BLK)
            return carry

        lax.fori_loop(0, blocks, block, 0)
        return j + blocks

    lax.fori_loop(0, 16, completion, 0)


def main_kernel(
    blk, nval, q, ck, cv, pk, pv, res, w, out,
    kv, wbuf, qv, rv, qf, rf, oown, mown, lown, scores, qc, oc, mc, lc, vc, rc,
    ctx, d2s, d2r, bs, br, ds, rx,
    q_sem, r_sem, kv_loc, kv_send, kv_recv, fw_send, fw_recv, w_loc, w_send, w_recv,
    c_send, c_recv, d2_send, d2_recv, b_send, b_recv, x_send, x_recv,
):
    x, zl, c, y, zh = position()
    oth = 1 - c
    bulk = zl * NX + x

    def bulk_at(dx, dz):
        return lax.rem(zl + dz, NZL) * NX + lax.rem(x + dx, NX)

    def tp_at(dzh, dy, core):
        return (lax.rem(zh + dzh, NZH) * NY + lax.rem(y + dy, NY)) * NC + core

    def remote(src, dst, send, recv, where):
        return pltpu.make_async_remote_copy(
            src_ref=src, dst_ref=dst, send_sem=send, recv_sem=recv, device_id=where, device_id_type=MESH
        )

    q_copy = pltpu.make_async_copy(q, qv, q_sem)
    r_copy = pltpu.make_async_copy(res, rv, r_sem)
    q_copy.start()
    r_copy.start()

    barrier = pltpu.get_barrier_semaphore()
    peers = [(bulk, tp_at(dzh, dy, c)) for dzh in range(NZH) for dy in range(NY) if dzh or dy]
    peers += [(bulk, tp_at(0, 0, oth))]
    peers += [
        (bulk_at(dx, dz), tp_at(dzh, 0, c))
        for dx in range(NX)
        for dz in range(NZL)
        for dzh in range(NZH)
        if dx or dz
    ]
    for where in peers:
        pl.semaphore_signal(barrier, inc=1, device_id=where, device_id_type=MESH)
    pl.semaphore_wait(barrier, len(peers))

    parts = (
        (pk.at[0], 0, 128),
        (pv.at[0], 128, 128),
        (ck, 256, 64),
        (cv, 320, 64),
    )

    def kv_copies(j):
        dzh, dy = j // NY, j % NY
        head = pl.multiple_of((lax.rem(zh + dzh, NZH) * NY + lax.rem(y + dy, NY)) * HD, HD)
        made = []
        for n, (src, at, rows) in enumerate(parts):
            s = src.at[:, pl.ds(head, HD)]
            d = kv.at[j, c, pl.ds(at, rows), :]
            if j == 0:
                made.append(pltpu.make_async_copy(s, d, kv_loc.at[n]))
            else:
                made.append(remote(s, d, kv_send.at[j, n], kv_recv.at[j, n], (bulk, tp_at(dzh, dy, c))))
        return made

    for j in (6, 5, 7, 4, 2, 1, 3, 0):
        for copy in kv_copies(j):
            copy.start()

    def w_copies(n):
        here = pltpu.make_async_copy(
            w.at[:, pl.ds(pl.multiple_of((2 * n + c) * FE, FE), FE)], wbuf.at[c, n], w_loc.at[n]
        )
        away = remote(
            w.at[:, pl.ds(pl.multiple_of((2 * n + oth) * FE, FE), FE)],
            wbuf.at[c, n],
            w_send.at[n],
            w_recv.at[n],
            (bulk, tp_at(0, 0, oth)),
        )
        return here, away

    for n in range(8):
        for copy in w_copies(n):
            copy.start()

    q_copy.wait()
    r_copy.wait()

    def widen(i, carry):
        rows = pl.ds(pl.multiple_of(i * 64, 64), 64)
        at = pl.ds(i * 8, 8)
        qf[at] = qv[rows, :].astype(F32).reshape(8, 8, FE)
        rf[at] = rv[rows, :].astype(F32).reshape(8, 8, FE)
        return carry

    lax.fori_loop(0, 16, widen, 0)

    def own_part(j, core):
        dzh, dy = lax.div(j, NY), lax.rem(j, NY)
        i = (lax.rem(zh + NZH - dzh, NZH) * NY + lax.rem(y + NY - dy, NY)) * NC + core
        rows = pl.ds(pl.multiple_of(i * 64, 64), 64)
        at = pl.ds(i * 8, 8)
        qs = jnp.concatenate([qv[rows, h * HD : (h + 1) * HD] for h in range(LH)], axis=0)
        s = lax.dot_general(qs, kv[j, core, 256:320, :], NT, preferred_element_type=F32) * SCALE
        row = lax.broadcasted_iota(jnp.int32, s.shape, 0) & 63
        col = lax.broadcasted_iota(jnp.int32, s.shape, 1)
        s = jnp.where(col <= row, s, -1e30)
        m = jnp.max(s, axis=1, keepdims=True)
        e = jnp.exp2(s - m)
        total = jnp.sum(e, axis=1, keepdims=True)
        o = jnp.dot(e.astype(BF16), kv[j, core, 320:384, :], preferred_element_type=F32)
        m, total = jnp.broadcast_to(m, o.shape), jnp.broadcast_to(total, o.shape)
        for h in range(LH):
            cols = slice(h * HD, (h + 1) * HD)
            part = slice(h * 64, (h + 1) * 64)
            oown[at, :, cols] = o[part].reshape(8, 8, HD)
            mown[at, :, cols] = m[part].reshape(8, 8, HD)
            lown[at, :, cols] = total[part].reshape(8, 8, HD)

    def forward(j):
        slot = kv.at[j, c]
        return remote(slot, slot, fw_send.at[j], fw_recv.at[j], (bulk, tp_at(0, 0, oth)))

    def from_sibling(j):
        slot = kv.at[j, oth]
        return remote(slot, slot, fw_send.at[j], fw_recv.at[j], (bulk, tp_at(0, 0, oth)))

    for j in (0, 1, 3, 2, 4, 5, 7, 6):
        for copy in kv_copies(j):
            if j == 0:
                copy.wait()
            else:
                copy.wait_recv()
        forward(j).start()
        own_part(j, c)

    def second(j, carry):
        from_sibling(j).wait_recv()
        own_part(j, oth)
        return carry

    lax.fori_loop(0, 8, second, 0)


    def attend(k):
        def gather(i, carry):
            b = blk[k * 16 + i]
            n = nval[k * 16 + i]
            at = pl.ds(pl.multiple_of(i * 8, 8), 8)
            qb, ob, mb, lb = qf[b], oown[b], mown[b], lown[b]
            for h in range(LH):
                cols = slice(h * HD, (h + 1) * HD)
                qc[h, at, :] = qb[:, cols]
                oc[h, at, :] = ob[:, cols]
                mc[h, at, :] = mb[:, cols]
                lc[h, at, :] = lb[:, cols]
            vc[at, :] = (lax.broadcasted_iota(jnp.int32, (8, HD), 0) < n).astype(F32)
            return carry

        lax.fori_loop(0, 16, gather, 0)

        for u in range(2):
            two = slice(2 * u, 2 * u + 2)
            qb = qc[two].reshape(2 * CR, HD).astype(BF16)
            top = None
            for j in range(8):
                s = lax.dot_general(
                    qb, kv[j, :, 0:128, :].reshape(256, HD), NT, preferred_element_type=F32
                )
                scores[j] = s
                both = jnp.maximum(s[:, :HD], s[:, HD:])
                top = both if top is None else jnp.maximum(top, both)
            m_own = mc[two].reshape(2 * CR, HD)
            m = jnp.maximum(jnp.max(top, axis=1, keepdims=True) * SCALE, m_own)
            wide = jnp.concatenate([m, m], axis=1)
            acc = jnp.zeros((2 * CR, HD), F32)
            sums = jnp.zeros((2 * CR, HD), F32)
            for j in range(8):
                e = jnp.exp2(scores[j] * SCALE - wide)
                sums = sums + (e[:, :HD] + e[:, HD:])
                acc = acc + jnp.dot(
                    e.astype(BF16), kv[j, :, 128:256, :].reshape(256, HD), preferred_element_type=F32
                )
            a = jnp.exp2(m_own - m)
            total = jnp.sum(sums, axis=1, keepdims=True) + a * lc[two].reshape(2 * CR, HD)
            o = (acc + a * oc[two].reshape(2 * CR, HD)) / total
            good = vc[...] > 0.5
            for h in range(2):
                v = jnp.where(good, o[h * CR : (h + 1) * CR], 0.0)
                ctx[k, c, :, (2 * u + h) * HD : (2 * u + h + 1) * HD] = v.astype(BF16)

    def ctx_copy(k, core):
        slot = ctx.at[k, core]
        return remote(slot, slot, c_send.at[k], c_recv.at[k], (bulk, tp_at(0, 0, oth)))

    def project(k, dy, dzh):
        n = lax.rem(zh + dzh, NZH) * NY + lax.rem(y + dy, NY)
        return jnp.dot(ctx[k, 0], wbuf[0, n], preferred_element_type=F32) + jnp.dot(
            ctx[k, 1], wbuf[1, n], preferred_element_type=F32
        )

    up, down = (bulk, tp_at(0, 1, c)), (bulk, tp_at(0, 3, c))
    toward = (up, down)

    def d2_copy(k, side):
        return remote(
            d2s.at[k, side], d2r.at[k, side], d2_send.at[k, side], d2_recv.at[k, side], toward[side]
        )

    def b_copy(k, side, dzh):
        return remote(
            bs.at[k, side, dzh],
            br.at[k, side, dzh],
            b_send.at[k, side, dzh],
            b_recv.at[k, side, dzh],
            toward[side],
        )

    def first_sends(k):
        ctx_copy(k, oth).wait_recv()
        for side in range(2):
            d2s[k, side] = project(k, 2, side).astype(BF16)
            d2_copy(k, side).start()
        for side in range(2):
            dzh = 1 - side
            bs[k, side, dzh] = project(k, 1 + 2 * side, dzh).astype(BF16)
            b_copy(k, side, dzh).start()

    def merged_sends(k):
        for side in range(2):
            mine = project(k, 1 + 2 * side, side)
            d2_copy(k, side).wait_recv()
            bs[k, side, side] = (mine + d2r[k, side].astype(F32)).astype(BF16)
            b_copy(k, side, side).start()

    def x_copy(k, dz, dzh):
        return remote(
            ds.at[k, dzh, pl.ds(dz * 32, 32), :],
            rx.at[k, dz, dzh],
            x_send.at[k, dz, dzh],
            x_recv.at[k, dz, dzh],
            (bulk_at(lax.rem(k + 1, NX), dz), tp_at(dzh, 0, c)),
        )

    def finish(k):
        def gather(i, carry):
            b = blk[k * 16 + i]
            n = nval[k * 16 + i]
            row = lax.broadcasted_iota(jnp.int32, (8, FE), 0)
            rc[pl.ds(pl.multiple_of(i * 8, 8), 8), :] = jnp.where(row < n, rf[b], 0.0)
            return carry

        lax.fori_loop(0, 16, gather, 0)
        for dzh in range(NZH):
            mine = project(k, 0, dzh)
            if dzh == 0:
                mine = mine + rc[...]
            for side in range(2):
                b_copy(k, side, dzh).wait_recv()
                mine = mine + br[k, side, dzh].astype(F32)
            ds[k, dzh] = mine.astype(BF16)
        for dzh in range(NZH):
            for dz in range(NZL):
                if dz or dzh:
                    x_copy(k, dz, dzh).start()
                else:

                    @pl.when(k < NK - 1)
                    def _():
                        x_copy(k, 0, 0).start()

    def w_from_sibling(n):
        return remote(
            w.at[:, pl.ds(0, FE)], wbuf.at[oth, n], w_send.at[n], w_recv.at[n], (bulk, tp_at(0, 0, oth))
        )

    def weights(n, carry):
        pltpu.make_async_copy(w.at[:, pl.ds(0, FE)], wbuf.at[c, n], w_loc.at[n]).wait()
        w_from_sibling(n).wait_recv()
        return carry

    def step(k, carry):
        @pl.when(k < NK)
        def _():
            attend(k)
            ctx_copy(k, c).start()

        @pl.when(k == 0)
        def _():
            lax.fori_loop(0, 8, weights, 0)

        @pl.when(k > 0)
        def _():
            merged_sends(k - 1)

        @pl.when(k < NK)
        def _():
            first_sends(k)

        @pl.when(k > 0)
        def _():
            finish(k - 1)

        return carry

    lax.fori_loop(0, NK + 1, step, 0)

    def collect(k, carry):
        dx = lax.rem(k + 1, NX)
        for dz in range(NZL):
            s = lax.rem(zl + NZL - dz, NZL) * NX + lax.rem(x + NX - dx, NX)
            x_copy(k, dz, 1).wait_recv()
            total = rx[k, dz, 1].astype(F32)
            if dz:
                x_copy(k, dz, 0).wait_recv()
            else:

                @pl.when(k < NK - 1)
                def _():
                    x_copy(k, 0, 0).wait_recv()

                @pl.when(k == NK - 1)
                def _():
                    rx[k, 0, 0] = ds[k, 0, 0:32, :]

            total = total + rx[k, dz, 0].astype(F32)
            out[pl.ds(pl.multiple_of(s * 32, 32), 32), :] = total.astype(BF16)
        return carry

    lax.fori_loop(0, NK, collect, 0)

    for j in range(1, 8):
        for copy in kv_copies(j):
            copy.wait_send()

    def left(n, carry):
        forward(n).wait_send()
        w_from_sibling(n).wait_send()
        return carry

    lax.fori_loop(0, 8, left, 0)

    def left_k(k, carry):
        ctx_copy(k, c).wait_send()
        for side in range(2):
            d2_copy(k, side).wait_send()
            for dzh in range(NZH):
                b_copy(k, side, dzh).wait_send()
        for dz in range(NZL):
            for dzh in range(NZH):
                if dz or dzh:
                    x_copy(k, dz, dzh).wait_send()
                else:

                    @pl.when(k < NK - 1)
                    def _():
                        x_copy(k, 0, 0).wait_send()

        return carry

    lax.fori_loop(0, NK, left_k, 0)


def local(queries, comp_keys, comp_values, prefix_keys, prefix_values, lengths, routing, residual, out_weight):
    smem = pl.BlockSpec(memory_space=pltpu.SMEM)
    anywhere = pl.BlockSpec(memory_space=pl.ANY)
    blk, nval = pl.pallas_call(
        tables_kernel,
        out_shape=[jax.ShapeDtypeStruct((64,), jnp.int32)] * 2,
        in_specs=[smem, smem],
        out_specs=[smem, smem],
        scratch_shapes=[pltpu.SMEM((16,), jnp.int32)],
        name="tables",
    )(lengths, routing)
    vmem = pltpu.VMEM
    dma = pltpu.SemaphoreType.DMA
    return pl.pallas_call(
        main_kernel,
        out_shape=jax.ShapeDtypeStruct((512, FE), BF16),
        in_specs=[smem, smem] + [anywhere] * 7,
        out_specs=pl.BlockSpec(memory_space=pltpu.VMEM),
        scratch_shapes=[
            vmem((8, 2, 384, HD), BF16),
            vmem((2, 8, 512, FE), BF16),
            vmem((1024, FE), BF16),
            vmem((1024, FE), BF16),
            vmem((128, 8, FE), F32),
            vmem((128, 8, FE), F32),
            vmem((128, 8, FE), F32),
            vmem((128, 8, FE), F32),
            vmem((128, 8, FE), F32),
            vmem((8, 2 * CR, 256), F32),
            vmem((LH, CR, HD), F32),
            vmem((LH, CR, HD), F32),
            vmem((LH, CR, HD), F32),
            vmem((LH, CR, HD), F32),
            vmem((CR, HD), F32),
            vmem((CR, FE), F32),
            vmem((NK, 2, CR, FE), BF16),
            vmem((NK, 2, CR, FE), BF16),
            vmem((NK, 2, CR, FE), BF16),
            vmem((NK, 2, 2, CR, FE), BF16),
            vmem((NK, 2, 2, CR, FE), BF16),
            vmem((NK, 2, CR, FE), BF16),
            vmem((NK, NZL, 2, 32, FE), BF16),
            dma, dma, dma((4,)), dma((8, 4)), dma((8, 4)), dma((8,)), dma((8,)),
            dma((8,)), dma((8,)), dma((8,)),
            dma((NK,)), dma((NK,)), dma((NK, 2)), dma((NK, 2)), dma((NK, 2, 2)), dma((NK, 2, 2)),
            dma((NK, NZL, 2)), dma((NK, NZL, 2)),
        ],
        compiler_params=pltpu.CompilerParams(
            collective_id=0, has_side_effects=True, vmem_limit_bytes=56 * 2**20
        ),
        name="attend_project_send",
    )(blk, nval, queries, comp_keys, comp_values, prefix_keys, prefix_values, residual, out_weight)


def solution(mesh):
    return jax.shard_map(
        local,
        mesh=mesh,
        in_specs=(
            P("bulk", "tp"),
            P(("bulk", "tp"), None),
            P(("bulk", "tp"), None),
            P("bulk", "tp", None),
            P("bulk", "tp", None),
            P("bulk", None),
            P("bulk", None),
            P("bulk", "tp"),
            P("tp", None),
        ),
        out_specs=P("bulk", "tp"),
        check_vma=False,
    )
```

time: 340 us -> 94.2 us (0.28)
  waiting for transfers between devices: 173 us -> 0 us
  Pallas kernels: 0 us -> 90.7 us
  matrix products: 42.3 us -> 0 us
  blocking collectives: 36.6 us -> 0 us
  other arithmetic: 26.4 us -> 0 us
  starting transfers between devices: 25.9 us -> 0 us
  local copies, waits for them, and re-layouts: 20 us -> 1.87 us
  between operations: 13.6 us -> 0.02 us
    reduce_scatter x1 -> x0, waiting for transfers between devices: 143 us -> none  [project(): lax.psum_scatter(lax.dot_general(out_weight, context, (((0,), (1,)), ((),...]
    pallas_call x0 -> x2, Pallas kernels: none -> 90.7 us  [the longest x1 88.3 us: local(): pl.pallas_call(main_kernel, out_shape=jax.ShapeDtypeStruct((512, FE), BF1...]
    dot_general x33 -> x0, matrix products: 42.3 us -> none  [the longest x8 15.8 us: attend(): jnp.einsum('bckqp,pkh->bckqh', expo_pre.astype(jnp.bfloat16), value_pre,...]
    all_to_all x1 -> x0, blocking collectives: 36.6 us -> none  [side_by_side(): lax.all_to_all(both, axis, split_axis=split_dim, concat_axis=concat_dim,...]
    all_to_all x4 -> x0, waiting for transfers between devices: 29.8 us -> none  [the longest x1 13.7 us: local(): lax.all_to_all(spread(prefix_keys), 'tp', split_axis=1, concat_axis=0, ti...]
    all_to_all x4 -> x0, starting transfers between devices: 25.9 us -> none  [the longest x1 11.3 us: local(): lax.all_to_all(spread(comp_keys), 'tp', split_axis=1, concat_axis=0, tile...]
    reduce_sum x19 -> x0, other arithmetic: 7.68 us -> none  [the longest x16 7.29 us: attend(): total = jnp.sum(expo_pre, axis=-1) + jnp.sum(expo_own, axis=-1)]
    gather x7 -> x0, local copies, waits for them, and re-layouts: 7.3 us -> none  [the longest x4 5.41 us: spread(): picked = cache.reshape(-1, KVH, HD)[:, head_table, :]]
  transfers between devices with their start and end apart: 5 -> 0, of which waited for: 4 -> 0; matrix products, arithmetic and copies ran while one was open for 7% -> 0% of each run, Pallas kernels for 0% -> 0%
where the time goes in v1:
time: 94.2 us; the launch traced here: 92.6 us
  Pallas kernels  90.7 us (96%)
  local copies, waits for them, and re-layouts  1.87 us (2%)
    pallas_call x1, Pallas kernels, local(): pl.pallas_call(main_kernel, out_shape=jax.ShapeDtypeStruct((512, FE), BF1...  88.3 us
    pallas_call x1, Pallas kernels, local(): pl.pallas_call(tables_kernel, out_shape=[jax.ShapeDtypeStruct((64,), jnp....  2.45 us

profile of v1, /device:TPU:2, one launch (start us, length us, event | category | flops | bytes accessed | tf_op | source)
XLA Modules:
  0.0 92.6 jit_solution(5067635431274959764)
XLA Ops:
  0.0 2.4 %tables.1 = (s32[64]{0:T(128)}, s32[64]{0:T(128)}) custom-call(s32[1,16]{1,0:T(1,128)} %lens.1, s32[1,64]{1,0:T(1,128)} %route.1), custom_call_target="tpu_custom_call" | custom-call | tf_op jit(solution)/shard_map/tables/pallas_call | solution.py:430
  2.5 88.3 %attend_project_send.1 = bf16[512,512]{1,0:T(8,128)(2,1)} custom-call(s32[64]{0:T(128)} %get-tuple-element.7.blk, s32[64]{0:T(128)} %get-tuple-element.8.nval, bf16[1024,512]{1,0:T(8,128)(2,1)} %q.1, bf16[64,1024]{1,0:T(8,128)(2,1)} %ck.1, bf16[64,1024]{1,0:T(8,128)(2,1)} %cv.1, bf16[1,128,1024]{2,1,0:T(8,128)(2,1)} %pk.1, bf16[1,128,1024]{2,1,0:T(8,128)(2,1)} %pv.1, ...), custom_call_target="tpu_custom_call" | custom-call | tf_op jit(solution)/shard_map/attend_project_send/pallas_call | solution.py:440
  90.7 1.9 %copy.11 = bf16[512,512]{1,0:T(8,128)(2,1)} copy(bf16[512,512]{1,0:T(8,128)(2,1)} %attend_project_send.1) | data formatting | bytes 1048576

commit v2 on v1

v2 whole, which is shorter than its diff:
```python
import math

import jax
import jax.numpy as jnp
from jax import lax
from jax.experimental import pallas as pl
from jax.experimental.pallas import tpu as pltpu
from jax.sharding import PartitionSpec as P

HD = 128
BLK = 8
NX, NY, NZL, NZH, NC = 4, 4, 4, 2, 2
NK = 4
DZ = NX * NZL // NK
CR = 512 // NK
CB = CR // BLK
LH = 4
FE = 512
SCALE = math.log2(math.e) / math.sqrt(HD)
F32, BF16 = jnp.float32, jnp.bfloat16
MESH = pl.DeviceIdType.MESH
NT = (((1,), (1,)), ((), ()))


def position():
    b, t = lax.axis_index("bulk"), lax.axis_index("tp")
    x, zl = lax.rem(b, NX), lax.div(b, NX)
    c, y, zh = lax.rem(t, NC), lax.rem(lax.div(t, NC), NY), lax.div(t, NC * NY)
    return x, zl, c, y, zh


def tables(lens, route, x, zl):
    sub = lax.broadcasted_iota(jnp.int32, (128, 128), 0)
    lane = lax.broadcasted_iota(jnp.int32, (128, 128), 1)
    size = jnp.zeros((128, 128), jnp.int32)
    for i in range(16):
        size = jnp.where((sub >> 3) == i, lens[0, i], size)
    first = (sub & 7) * BLK
    live = first < size
    one = jnp.where(live, 1, 0)
    rank = jnp.sum(jnp.where(sub < lane, one, 0), axis=0, keepdims=True)
    rank = jnp.sum(jnp.where(sub == lane, rank, 0), axis=1, keepdims=True)
    place = lax.broadcasted_iota(jnp.int32, (8, 128), 1)
    dest = jnp.full((8, 128), -1, jnp.int32)
    for j in range(64):
        dest = jnp.where(place == j, route[0, j], dest)
    dest = dest[0:1]
    down = jnp.sum(jnp.where(sub == lane, dest, 0), axis=1, keepdims=True)
    seen = jnp.sum(jnp.where((down == dest) & (sub < lane), 1, 0), axis=0, keepdims=True)
    k = ((dest & 3) - x + 2 * NX - 1) & 3
    dz = ((dest >> 2) - zl + NZL) & 3
    slot = (k * NZL + dz) * 4 + seen
    slot = jnp.sum(jnp.where((rank == lane) & live, slot, 0), axis=1, keepdims=True)
    here = (slot == lane) & live
    blk = jnp.sum(jnp.where(here, sub, 0), axis=0, keepdims=True)
    nval = jnp.sum(jnp.where(here, jnp.minimum(size - first, BLK), 0), axis=0, keepdims=True)
    return blk, nval


def main_kernel(
    lens, route, q, ck, cv, pk, pv, res, w, out0, out1,
    kv, wbuf, qv, rv, qf, rf, oown, mown, lown, scores, qc, oc, mc, lc, vc, rc,
    ctx, d2s, d2r, bs, br, ds, tab, order, met,
    t_sem, q_sem, r_sem, kv_loc, kv_send, kv_recv, fw_send, fw_recv, w_loc, w_send, w_recv,
    c_send, c_recv, d2_send, d2_recv, b_send, b_recv, x_send, x_recv,
):
    x, zl, c, y, zh = position()
    oth = 1 - c
    bulk = zl * NX + x

    def bulk_at(dx, dz):
        return lax.rem(zl + dz, NZL) * NX + lax.rem(x + dx, NX)

    def tp_at(dzh, dy, core):
        return (lax.rem(zh + dzh, NZH) * NY + lax.rem(y + dy, NY)) * NC + core

    def remote(src, dst, send, recv, where):
        return pltpu.make_async_remote_copy(
            src_ref=src, dst_ref=dst, send_sem=send, recv_sem=recv, device_id=where, device_id_type=MESH
        )

    q_copy = pltpu.make_async_copy(q, qv, q_sem)
    r_copy = pltpu.make_async_copy(res, rv, r_sem)
    q_copy.start()
    r_copy.start()

    barrier = pltpu.get_barrier_semaphore()
    peers = [(bulk, tp_at(dzh, dy, c)) for dzh in range(NZH) for dy in range(NY) if dzh or dy]
    peers += [(bulk, tp_at(0, 0, oth))]
    x_line = [(bulk_at(dx, 0), tp_at(0, 0, c)) for dx in (1, 3, 2)]
    z = zh * NZL + zl

    def z_at(dz):
        at = lax.rem(z + dz, NZH * NZL)
        return lax.rem(at, NZL) * NX + x, (lax.div(at, NZL) * NY + y) * NC + c

    z_near = [z_at(1), z_at(7)]
    peers += x_line[:2] + z_near
    for where in peers:
        pl.semaphore_signal(barrier, inc=1, device_id=where, device_id_type=MESH)
    pl.semaphore_wait(barrier, len(peers))

    parts = (
        (pk.at[0], 0, 128),
        (pv.at[0], 128, 128),
        (ck, 256, 64),
        (cv, 320, 64),
    )

    def kv_copies(j, chosen=range(4)):
        dzh, dy = j // NY, j % NY
        head = pl.multiple_of((lax.rem(zh + dzh, NZH) * NY + lax.rem(y + dy, NY)) * HD, HD)
        made = []
        for n in chosen:
            src, at, rows = parts[n]
            s = src.at[:, pl.ds(head, HD)]
            d = kv.at[j, c, pl.ds(at, rows), :]
            if j == 0:
                made.append(pltpu.make_async_copy(s, d, kv_loc.at[n]))
            else:
                made.append(remote(s, d, kv_send.at[j, n], kv_recv.at[j, n], (bulk, tp_at(dzh, dy, c))))
        return made

    for few in ((2, 3), (0, 1)):
        for j in (6, 5, 7, 4, 2, 1, 3, 0):
            for copy in kv_copies(j, few):
                copy.start()

    def w_copies(n):
        here = pltpu.make_async_copy(
            w.at[:, pl.ds(pl.multiple_of((2 * n + c) * FE, FE), FE)], wbuf.at[c, n], w_loc.at[n]
        )
        away = remote(
            w.at[:, pl.ds(pl.multiple_of((2 * n + oth) * FE, FE), FE)],
            wbuf.at[c, n],
            w_send.at[n],
            w_recv.at[n],
            (bulk, tp_at(0, 0, oth)),
        )
        return here, away

    for n in range(8):
        for copy in w_copies(n):
            copy.start()

    for n, known in enumerate((x_line[:2], z_near, z_near, x_line)):
        for where in known:
            pl.semaphore_signal(met.at[n], inc=1, device_id=where, device_id_type=MESH)
        pl.semaphore_wait(met.at[n], len(known))

    blk, nval = tables(lens, route, x, zl)
    tab[0:1, :] = blk
    tab[1:2, :] = nval
    t_copy = pltpu.make_async_copy(tab, order, t_sem)
    t_copy.start()
    q_copy.wait()
    r_copy.wait()
    t_copy.wait()

    def widen(i, carry):
        rows = pl.ds(pl.multiple_of(i * 64, 64), 64)
        at = pl.ds(i * 8, 8)
        qf[at] = qv[rows, :].astype(F32).reshape(8, 8, FE)
        rf[at] = rv[rows, :].astype(F32).reshape(8, 8, FE)
        return carry

    lax.fori_loop(0, 16, widen, 0)

    def own_part(j, core):
        dzh, dy = lax.div(j, NY), lax.rem(j, NY)
        i = (lax.rem(zh + NZH - dzh, NZH) * NY + lax.rem(y + NY - dy, NY)) * NC + core
        rows = pl.ds(pl.multiple_of(i * 64, 64), 64)
        at = pl.ds(i * 8, 8)
        qs = jnp.concatenate([qv[rows, h * HD : (h + 1) * HD] for h in range(LH)], axis=0)
        s = lax.dot_general(qs, kv[j, core, 256:320, :], NT, preferred_element_type=F32) * SCALE
        row = lax.broadcasted_iota(jnp.int32, s.shape, 0) & 63
        col = lax.broadcasted_iota(jnp.int32, s.shape, 1)
        s = jnp.where(col <= row, s, -1e30)
        m = jnp.max(s, axis=1, keepdims=True)
        e = jnp.exp2(s - m)
        total = jnp.sum(e, axis=1, keepdims=True)
        o = jnp.dot(e.astype(BF16), kv[j, core, 320:384, :], preferred_element_type=F32)
        m, total = jnp.broadcast_to(m, o.shape), jnp.broadcast_to(total, o.shape)
        for h in range(LH):
            cols = slice(h * HD, (h + 1) * HD)
            part = slice(h * 64, (h + 1) * 64)
            oown[at, :, cols] = o[part].reshape(8, 8, HD)
            mown[at, :, cols] = m[part].reshape(8, 8, HD)
            lown[at, :, cols] = total[part].reshape(8, 8, HD)

    pieces = (pl.ds(0, 256), pl.ds(256, 128))

    def forward(j, n):
        part = kv.at[j, c, pieces[n], :]
        return remote(part, part, fw_send.at[j, n], fw_recv.at[j, n], (bulk, tp_at(0, 0, oth)))

    def from_sibling(j, n):
        part = kv.at[j, oth, pieces[n], :]
        return remote(part, part, fw_send.at[j, n], fw_recv.at[j, n], (bulk, tp_at(0, 0, oth)))

    def arrived(j, n):
        for copy in kv_copies(j, (2 * n, 2 * n + 1)):
            if j == 0:
                copy.wait()
            else:
                copy.wait_recv()
        forward(j, n).start()

    near, late = (0, 1, 3, 2), (4, 5, 7, 6)
    for some in (near, late):
        for j in some:
            arrived(j, 1)
            own_part(j, c)
        for j in some:
            from_sibling(j, 1).wait_recv()
            own_part(j, oth)
    for j in near + late:
        arrived(j, 0)
    for j in near + late:
        from_sibling(j, 0).wait_recv()

    def attend(k):
        def gather(i, carry):
            b = order[0, k * CB + i]
            n = order[1, k * CB + i]
            at = pl.ds(pl.multiple_of(i * 8, 8), 8)
            qb, ob, mb, lb = qf[b], oown[b], mown[b], lown[b]
            for h in range(LH):
                cols = slice(h * HD, (h + 1) * HD)
                qc[h, at, :] = qb[:, cols]
                oc[h, at, :] = ob[:, cols]
                mc[h, at, :] = mb[:, cols]
                lc[h, at, :] = lb[:, cols]
            vc[at, :] = (lax.broadcasted_iota(jnp.int32, (8, HD), 0) < n).astype(F32)
            return carry

        lax.fori_loop(0, CB, gather, 0)

        rows = LH * CR
        qb = qc[...].reshape(rows, HD).astype(BF16)
        top = None
        for j in range(8):
            s = lax.dot_general(
                qb, kv[j, :, 0:128, :].reshape(256, HD), NT, preferred_element_type=F32
            )
            scores[j] = s
            both = jnp.maximum(s[:, :HD], s[:, HD:])
            top = both if top is None else jnp.maximum(top, both)
        m_own = mc[...].reshape(rows, HD)
        m = jnp.maximum(jnp.max(top, axis=1, keepdims=True) * SCALE, m_own)
        wide = jnp.concatenate([m, m], axis=1)
        acc = jnp.zeros((rows, HD), F32)
        sums = jnp.zeros((rows, HD), F32)
        for j in range(8):
            e = jnp.exp2(scores[j] * SCALE - wide)
            sums = sums + (e[:, :HD] + e[:, HD:])
            acc = acc + jnp.dot(
                e.astype(BF16), kv[j, :, 128:256, :].reshape(256, HD), preferred_element_type=F32
            )
        a = jnp.exp2(m_own - m)
        total = jnp.sum(sums, axis=1, keepdims=True) + a * lc[...].reshape(rows, HD)
        o = (acc + a * oc[...].reshape(rows, HD)) / total
        good = vc[...] > 0.5
        for h in range(LH):
            v = jnp.where(good, o[h * CR : (h + 1) * CR], 0.0)
            ctx[k, c, :, h * HD : (h + 1) * HD] = v.astype(BF16)

    def ctx_copy(k, core):
        slot = ctx.at[k, core]
        return remote(slot, slot, c_send.at[k], c_recv.at[k], (bulk, tp_at(0, 0, oth)))

    def project(k, dy, dzh):
        n = lax.rem(zh + dzh, NZH) * NY + lax.rem(y + dy, NY)
        return jnp.dot(ctx[k, 0], wbuf[0, n], preferred_element_type=F32) + jnp.dot(
            ctx[k, 1], wbuf[1, n], preferred_element_type=F32
        )

    up, down = (bulk, tp_at(0, 1, c)), (bulk, tp_at(0, 3, c))
    toward = (up, down)

    def d2_copy(k, side):
        return remote(
            d2s.at[k, side], d2r.at[k, side], d2_send.at[k, side], d2_recv.at[k, side], toward[side]
        )

    def b_copy(k, side, dzh):
        return remote(
            bs.at[k, side, dzh],
            br.at[k, side, dzh],
            b_send.at[k, side, dzh],
            b_recv.at[k, side, dzh],
            toward[side],
        )

    def first_sends(k):
        ctx_copy(k, oth).wait_recv()
        for side in range(2):
            d2s[k, side] = project(k, 2, side).astype(BF16)
            d2_copy(k, side).start()
        for side in range(2):
            dzh = 1 - side
            bs[k, side, dzh] = project(k, 1 + 2 * side, dzh).astype(BF16)
            b_copy(k, side, dzh).start()

    def merged_sends(k):
        for side in range(2):
            mine = project(k, 1 + 2 * side, side)
            d2_copy(k, side).wait_recv()
            bs[k, side, side] = (mine + d2r[k, side].astype(F32)).astype(BF16)
            b_copy(k, side, side).start()

    mine32 = pl.ds(pl.multiple_of(bulk * 32, 32), 32)
    outs = (out0, out1)

    def x_copy(k, n, dzh):
        return remote(
            ds.at[k, dzh, pl.ds(n * 32, 32), :],
            outs[dzh].at[mine32, :],
            x_send.at[k, n, dzh],
            x_recv.at[k, n, dzh],
            (bulk_at(lax.rem(lax.div(k, NK // NX) + 1, NX), lax.rem(k, NK // NX) * DZ + n), tp_at(dzh, 0, c)),
        )

    def stay():
        return pltpu.make_async_copy(ds.at[NK - NK // NX, 0, 0:32, :], out0.at[mine32, :], q_sem)

    def x_each(k, do):
        for dzh in range(NZH):
            for n in range(DZ):
                if n or dzh:
                    do(x_copy(k, n, dzh))
                else:

                    @pl.when(k != NK - NK // NX)
                    def _():
                        do(x_copy(k, 0, 0))

    def finish(k):
        def gather(i, carry):
            b = order[0, k * CB + i]
            n = order[1, k * CB + i]
            row = lax.broadcasted_iota(jnp.int32, (8, FE), 0)
            rc[pl.ds(pl.multiple_of(i * 8, 8), 8), :] = jnp.where(row < n, rf[b], 0.0)
            return carry

        lax.fori_loop(0, CB, gather, 0)
        for dzh in range(NZH):
            mine = project(k, 0, dzh)
            if dzh == 0:
                mine = mine + rc[...]
            for side in range(2):
                b_copy(k, side, dzh).wait_recv()
                mine = mine + br[k, side, dzh].astype(F32)
            ds[k, dzh] = mine.astype(BF16)
        x_each(k, lambda copy: copy.start())

        @pl.when(k == NK - NK // NX)
        def _():
            stay().start()

    def w_from_sibling(n):
        return remote(
            w.at[:, pl.ds(0, FE)], wbuf.at[oth, n], w_send.at[n], w_recv.at[n], (bulk, tp_at(0, 0, oth))
        )

    def weights(n, carry):
        pltpu.make_async_copy(w.at[:, pl.ds(0, FE)], wbuf.at[c, n], w_loc.at[n]).wait()
        w_from_sibling(n).wait_recv()
        return carry

    def step(k, carry):
        @pl.when(k < NK)
        def _():
            attend(k)
            ctx_copy(k, c).start()

        @pl.when(k == 0)
        def _():
            lax.fori_loop(0, 8, weights, 0)

        @pl.when(k > 0)
        def _():
            merged_sends(k - 1)

        @pl.when(k < NK)
        def _():
            first_sends(k)

        @pl.when(k > 0)
        def _():
            finish(k - 1)

        return carry

    lax.fori_loop(0, NK + 1, step, 0)

    def collect(k, carry):
        x_each(k, lambda copy: copy.wait_recv())
        return carry

    lax.fori_loop(0, NK, collect, 0)
    stay().wait()

    for j in range(1, 8):
        for copy in kv_copies(j):
            copy.wait_send()

    def left(n, carry):
        for part in range(2):
            forward(n, part).wait_send()
        w_from_sibling(n).wait_send()
        return carry

    lax.fori_loop(0, 8, left, 0)

    def left_k(k, carry):
        ctx_copy(k, c).wait_send()
        for side in range(2):
            d2_copy(k, side).wait_send()
            for dzh in range(NZH):
                b_copy(k, side, dzh).wait_send()
        x_each(k, lambda copy: copy.wait_send())
        return carry

    lax.fori_loop(0, NK, left_k, 0)


def local(queries, comp_keys, comp_values, prefix_keys, prefix_values, lengths, routing, residual, out_weight):
    smem = pl.BlockSpec(memory_space=pltpu.SMEM)
    anywhere = pl.BlockSpec(memory_space=pl.ANY)
    vmem = pltpu.VMEM
    dma = pltpu.SemaphoreType.DMA
    near, far = pl.pallas_call(
        main_kernel,
        out_shape=[jax.ShapeDtypeStruct((512, FE), BF16)] * 2,
        in_specs=[smem, smem] + [anywhere] * 7,
        out_specs=[anywhere] * 2,
        scratch_shapes=[
            vmem((8, 2, 384, HD), BF16),
            vmem((2, 8, 512, FE), BF16),
            vmem((1024, FE), BF16),
            vmem((1024, FE), BF16),
            vmem((128, 8, FE), F32),
            vmem((128, 8, FE), F32),
            vmem((128, 8, FE), F32),
            vmem((128, 8, FE), F32),
            vmem((128, 8, FE), F32),
            vmem((8, LH * CR, 256), F32),
            vmem((LH, CR, HD), F32),
            vmem((LH, CR, HD), F32),
            vmem((LH, CR, HD), F32),
            vmem((LH, CR, HD), F32),
            vmem((CR, HD), F32),
            vmem((CR, FE), F32),
            vmem((NK, 2, CR, FE), BF16),
            vmem((NK, 2, CR, FE), BF16),
            vmem((NK, 2, CR, FE), BF16),
            vmem((NK, 2, 2, CR, FE), BF16),
            vmem((NK, 2, 2, CR, FE), BF16),
            vmem((NK, 2, CR, FE), BF16),
            vmem((8, 128), jnp.int32),
            pltpu.SMEM((8, 128), jnp.int32),
            pltpu.SemaphoreType.REGULAR((4,)),
            dma,
            dma, dma, dma((4,)), dma((8, 4)), dma((8, 4)), dma((8, 2)), dma((8, 2)),
            dma((8,)), dma((8,)), dma((8,)),
            dma((NK,)), dma((NK,)), dma((NK, 2)), dma((NK, 2)), dma((NK, 2, 2)), dma((NK, 2, 2)),
            dma((NK, DZ, 2)), dma((NK, DZ, 2)),
        ],
        compiler_params=pltpu.CompilerParams(
            collective_id=0, has_side_effects=True, vmem_limit_bytes=56 * 2**20
        ),
        name="attend_project_send",
    )(lengths, routing, queries, comp_keys, comp_values, prefix_keys, prefix_values, residual, out_weight)
    return (near.astype(F32) + far.astype(F32)).astype(BF16)


def solution(mesh):
    return jax.shard_map(
        local,
        mesh=mesh,
        in_specs=(
            P("bulk", "tp"),
            P(("bulk", "tp"), None),
            P(("bulk", "tp"), None),
            P("bulk", "tp", None),
            P("bulk", "tp", None),
            P("bulk", None),
            P("bulk", None),
            P("bulk", "tp"),
            P("tp", None),
        ),
        out_specs=P("bulk", "tp"),
        check_vma=False,
    )
```

time: 94.2 us -> 84.7 us (0.90); the launches traced: 92.6 us -> 84.6 us
  Pallas kernels: 90.7 us -> 82.4 us
  other arithmetic: 0 us -> 2.13 us
  local copies, waits for them, and re-layouts: 1.87 us -> 0 us
    pallas_call x2 -> x1, Pallas kernels: 90.7 us -> 82.4 us  [local(): pl.pallas_call(main_kernel, out_shape=[jax.ShapeDtypeStruct((512, FE), BF...]
    convert_element_type x0 -> x1, other arithmetic: none -> 2.13 us  [local(): return (near.astype(F32) + far.astype(F32)).astype(BF16)]
    unnamed x1 -> x0, local copies, waits for them, and re-layouts: 1.87 us -> none
where the time goes in v2:
time: 84.7 us; the launch traced here: 84.6 us
  Pallas kernels  82.4 us (97%)
  other arithmetic  2.13 us (3%)
    pallas_call x1, Pallas kernels, local(): pl.pallas_call(main_kernel, out_shape=[jax.ShapeDtypeStruct((512, FE), BF...  82.4 us
    convert_element_type x1, other arithmetic, local(): return (near.astype(F32) + far.astype(F32)).astype(BF16)  2.13 us

profile of v2, /device:TPU:2, one launch (start us, length us, event | category | flops | bytes accessed | tf_op | source)
XLA Modules:
  0.0 84.6 jit_solution(13592933362263991536)
XLA Ops:
  0.0 82.4 %attend_project_send.1 = (bf16[512,512]{1,0:T(8,128)(2,1)}, bf16[512,512]{1,0:T(8,128)(2,1)}) custom-call(s32[1,16]{1,0:T(1,128)} %lens.1, s32[1,64]{1,0:T(1,128)} %route.1, bf16[1024,512]{1,0:T(8,128)(2,1)} %q.1, bf16[64,1024]{1,0:T(8,128)(2,1)} %ck.1, bf16[64,1024]{1,0:T(8,128)(2,1)} %cv.1, bf16[1,128,1024]{2,1,0:T(8,128)(2,1)} %pk.1, ...), custom_call_target="tpu_custom_call" | custom-call | tf_op jit(solution)/shard_map/attend_project_send/pallas_call | solution.py:433
  82.4 2.1 %add_convert_fusion = bf16[512,512]{1,0:T(8,128)(2,1)} fusion(bf16[512,512]{1,0:T(8,128)(2,1)} %get-tuple-element.8, bf16[512,512]{1,0:T(8,128)(2,1)} %get-tuple-element.7), kind=kLoop, calls=%fused_computation | loop fusion | flops 1048576 | bytes 1572864 | tf_op jit(solution)/shard_map/convert_element_type | solution.py:475

commit v3 on v2

--- a/solution.py
+++ b/solution.py
@@ -58,7 +58,7 @@
 
 
 def main_kernel(
-    lens, route, q, ck, cv, pk, pv, res, w, out0, out1,
+    lens, route, q, ck, cv, pk, pv, res, w, out,
     kv, wbuf, qv, rv, qf, rf, oown, mown, lown, scores, qc, oc, mc, lc, vc, rc,
     ctx, d2s, d2r, bs, br, ds, tab, order, met,
     t_sem, q_sem, r_sem, kv_loc, kv_send, kv_recv, fw_send, fw_recv, w_loc, w_send, w_recv,
@@ -121,7 +121,7 @@
                 made.append(remote(s, d, kv_send.at[j, n], kv_recv.at[j, n], (bulk, tp_at(dzh, dy, c))))
         return made
 
-    for few in ((2, 3), (0, 1)):
+    for few in ((2, 3), (0,), (1,)):
         for j in (6, 5, 7, 4, 2, 1, 3, 0):
             for copy in kv_copies(j, few):
                 copy.start()
@@ -188,18 +188,18 @@
             mown[at, :, cols] = m[part].reshape(8, 8, HD)
             lown[at, :, cols] = total[part].reshape(8, 8, HD)
 
-    pieces = (pl.ds(0, 256), pl.ds(256, 128))
+    pieces = ((256, 128, (2, 3)), (0, 128, (0,)), (128, 128, (1,)))
 
     def forward(j, n):
-        part = kv.at[j, c, pieces[n], :]
+        part = kv.at[j, c, pl.ds(*pieces[n][:2]), :]
         return remote(part, part, fw_send.at[j, n], fw_recv.at[j, n], (bulk, tp_at(0, 0, oth)))
 
     def from_sibling(j, n):
-        part = kv.at[j, oth, pieces[n], :]
+        part = kv.at[j, oth, pl.ds(*pieces[n][:2]), :]
         return remote(part, part, fw_send.at[j, n], fw_recv.at[j, n], (bulk, tp_at(0, 0, oth)))
 
     def arrived(j, n):
-        for copy in kv_copies(j, (2 * n, 2 * n + 1)):
+        for copy in kv_copies(j, pieces[n][2]):
             if j == 0:
                 copy.wait()
             else:
@@ -209,17 +209,19 @@
     near, late = (0, 1, 3, 2), (4, 5, 7, 6)
     for some in (near, late):
         for j in some:
-            arrived(j, 1)
+            arrived(j, 0)
             own_part(j, c)
         for j in some:
-            from_sibling(j, 1).wait_recv()
+            from_sibling(j, 0).wait_recv()
             own_part(j, oth)
-    for j in near + late:
-        arrived(j, 0)
-    for j in near + late:
-        from_sibling(j, 0).wait_recv()
-
-    def attend(k):
+
+    def all_here(n):
+        for j in near + late:
+            arrived(j, n)
+        for j in near + late:
+            from_sibling(j, n).wait_recv()
+
+    def attend(k, first=False):
         def gather(i, carry):
             b = order[0, k * CB + i]
             n = order[1, k * CB + i]
@@ -236,6 +238,8 @@
 
         lax.fori_loop(0, CB, gather, 0)
 
+        if first:
+            all_here(1)
         rows = LH * CR
         qb = qc[...].reshape(rows, HD).astype(BF16)
         top = None
@@ -249,6 +253,8 @@
         m_own = mc[...].reshape(rows, HD)
         m = jnp.maximum(jnp.max(top, axis=1, keepdims=True) * SCALE, m_own)
         wide = jnp.concatenate([m, m], axis=1)
+        if first:
+            all_here(2)
         acc = jnp.zeros((rows, HD), F32)
         sums = jnp.zeros((rows, HD), F32)
         for j in range(8):
@@ -310,30 +316,32 @@
             b_copy(k, side, side).start()
 
     mine32 = pl.ds(pl.multiple_of(bulk * 32, 32), 32)
-    outs = (out0, out1)
 
     def x_copy(k, n, dzh):
         return remote(
             ds.at[k, dzh, pl.ds(n * 32, 32), :],
-            outs[dzh].at[mine32, :],
+            out.at[dzh, mine32, :],
             x_send.at[k, n, dzh],
             x_recv.at[k, n, dzh],
             (bulk_at(lax.rem(lax.div(k, NK // NX) + 1, NX), lax.rem(k, NK // NX) * DZ + n), tp_at(dzh, 0, c)),
         )
 
     def stay():
-        return pltpu.make_async_copy(ds.at[NK - NK // NX, 0, 0:32, :], out0.at[mine32, :], q_sem)
+        return pltpu.make_async_copy(ds.at[NK - NK // NX, 0, 0:32, :], out.at[0, mine32, :], q_sem)
+
+    def x_half(k, dzh, do):
+        for n in range(DZ):
+            if n or dzh:
+                do(x_copy(k, n, dzh))
+            else:
+
+                @pl.when(k != NK - NK // NX)
+                def _():
+                    do(x_copy(k, 0, 0))
 
     def x_each(k, do):
         for dzh in range(NZH):
-            for n in range(DZ):
-                if n or dzh:
-                    do(x_copy(k, n, dzh))
-                else:
-
-                    @pl.when(k != NK - NK // NX)
-                    def _():
-                        do(x_copy(k, 0, 0))
+            x_half(k, dzh, do)
 
     def finish(k):
         def gather(i, carry):
@@ -344,15 +352,15 @@
             return carry
 
         lax.fori_loop(0, CB, gather, 0)
-        for dzh in range(NZH):
+        for dzh in (1, 0):
             mine = project(k, 0, dzh)
             if dzh == 0:
                 mine = mine + rc[...]
-            for side in range(2):
+            for side in (1 - dzh, dzh):
                 b_copy(k, side, dzh).wait_recv()
                 mine = mine + br[k, side, dzh].astype(F32)
             ds[k, dzh] = mine.astype(BF16)
-        x_each(k, lambda copy: copy.start())
+            x_half(k, dzh, lambda copy: copy.start())
 
         @pl.when(k == NK - NK // NX)
         def _():
@@ -368,16 +376,11 @@
         w_from_sibling(n).wait_recv()
         return carry
 
+    attend(0, first=True)
+    ctx_copy(0, c).start()
+    lax.fori_loop(0, 8, weights, 0)
+
     def step(k, carry):
-        @pl.when(k < NK)
-        def _():
-            attend(k)
-            ctx_copy(k, c).start()
-
-        @pl.when(k == 0)
-        def _():
-            lax.fori_loop(0, 8, weights, 0)
-
         @pl.when(k > 0)
         def _():
             merged_sends(k - 1)
@@ -386,6 +389,11 @@
         def _():
             first_sends(k)
 
+        @pl.when(k < NK - 1)
+        def _():
+            attend(k + 1)
+            ctx_copy(k + 1, c).start()
+
         @pl.when(k > 0)
         def _():
             finish(k - 1)
@@ -406,7 +414,7 @@
             copy.wait_send()
 
     def left(n, carry):
-        for part in range(2):
+        for part in range(3):
             forward(n, part).wait_send()
         w_from_sibling(n).wait_send()
         return carry
@@ -430,11 +438,11 @@
     anywhere = pl.BlockSpec(memory_space=pl.ANY)
     vmem = pltpu.VMEM
     dma = pltpu.SemaphoreType.DMA
-    near, far = pl.pallas_call(
+    both = pl.pallas_call(
         main_kernel,
-        out_shape=[jax.ShapeDtypeStruct((512, FE), BF16)] * 2,
+        out_shape=pltpu.VMEM((NZH, 512, FE), BF16),
         in_specs=[smem, smem] + [anywhere] * 7,
-        out_specs=[anywhere] * 2,
+        out_specs=pl.BlockSpec(memory_space=pltpu.VMEM),
         scratch_shapes=[
             vmem((8, 2, 384, HD), BF16),
             vmem((2, 8, 512, FE), BF16),
@@ -462,7 +470,7 @@
             pltpu.SMEM((8, 128), jnp.int32),
             pltpu.SemaphoreType.REGULAR((4,)),
             dma,
-            dma, dma, dma((4,)), dma((8, 4)), dma((8, 4)), dma((8, 2)), dma((8, 2)),
+            dma, dma, dma((4,)), dma((8, 4)), dma((8, 4)), dma((8, 3)), dma((8, 3)),
             dma((8,)), dma((8,)), dma((8,)),
             dma((NK,)), dma((NK,)), dma((NK, 2)), dma((NK, 2)), dma((NK, 2, 2)), dma((NK, 2, 2)),
             dma((NK, DZ, 2)), dma((NK, DZ, 2)),
@@ -472,7 +480,7 @@
         ),
         name="attend_project_send",
     )(lengths, routing, queries, comp_keys, comp_values, prefix_keys, prefix_values, residual, out_weight)
-    return (near.astype(F32) + far.astype(F32)).astype(BF16)
+    return (both[0].astype(F32) + both[1].astype(F32)).astype(BF16)
 
 
 def solution(mesh):

time: 84.7 us -> 81 us (0.956)
  Pallas kernels: 82.4 us -> 79.4 us
  other arithmetic: 2.13 us -> 0.93 us
    pallas_call x1, Pallas kernels: 82.4 us -> 79.4 us  [local(): pl.pallas_call(main_kernel, out_shape=pltpu.VMEM((NZH, 512, FE), BF16), i...]
    convert_element_type x1, other arithmetic: 2.13 us -> 0.93 us  [local(): return (both[0].astype(F32) + both[1].astype(F32)).astype(BF16)]
where the time goes in v3:
time: 81 us; the launch traced here: 80.4 us
  Pallas kernels  79.4 us (98%)
  other arithmetic  0.93 us (1%)
    pallas_call x1, Pallas kernels, local(): pl.pallas_call(main_kernel, out_shape=pltpu.VMEM((NZH, 512, FE), BF16), i...  79.4 us

profile of v3, /device:TPU:2, one launch (start us, length us, event | category | flops | bytes accessed | tf_op | source)
XLA Modules:
  0.0 80.4 jit_solution(7431474647406861058)
XLA Ops:
  0.0 79.4 %attend_project_send.1 = bf16[2,512,512]{2,1,0:T(8,128)(2,1)S(1)} custom-call(s32[1,16]{1,0:T(1,128)} %lens.1, s32[1,64]{1,0:T(1,128)} %route.1, bf16[1024,512]{1,0:T(8,128)(2,1)} %q.1, bf16[64,1024]{1,0:T(8,128)(2,1)} %ck.1, bf16[64,1024]{1,0:T(8,128)(2,1)} %cv.1, bf16[1,128,1024]{2,1,0:T(8,128)(2,1)} %pk.1, bf16[1,128,1024]{2,1,0:T(8,128)(2,1)} %pv.1, ...), custom_call_target="tpu_custom_call" | custom-call | tf_op jit(solution)/shard_map/attend_project_send/pallas_call | solution.py:441
  79.4 0.9 %fusion = bf16[512,512]{1,0:T(8,128)(2,1)} fusion(bf16[2,512,512]{2,1,0:T(8,128)(2,1)S(1)} %attend_project_send.1), kind=kLoop, calls=%fused_computation.1 | loop fusion | flops 1048576 | bytes 1572864 | tf_op jit(solution)/shard_map/convert_element_type | solution.py:483

commit v4 on v3

--- a/solution.py
+++ b/solution.py
@@ -10,10 +10,13 @@
 HD = 128
 BLK = 8
 NX, NY, NZL, NZH, NC = 4, 4, 4, 2, 2
-NK = 4
-DZ = NX * NZL // NK
-CR = 512 // NK
-CB = CR // BLK
+SEND = 32
+CHUNKS = (96, 160, 160, 96)
+NK = len(CHUNKS)
+STARTS = tuple(sum(CHUNKS[:k]) for k in range(NK))
+CR = max(CHUNKS)
+ND = NX * NZL
+STAYS = ND - NZL
 LH = 4
 FE = 512
 SCALE = math.log2(math.e) / math.sqrt(HD)
@@ -95,7 +98,7 @@
         return lax.rem(at, NZL) * NX + x, (lax.div(at, NZL) * NY + y) * NC + c
 
     z_near = [z_at(1), z_at(7)]
-    peers += x_line[:2] + z_near
+    peers += [x_line[1], z_near[1]]
     for where in peers:
         pl.semaphore_signal(barrier, inc=1, device_id=where, device_id_type=MESH)
     pl.semaphore_wait(barrier, len(peers))
@@ -143,7 +146,9 @@
         for copy in w_copies(n):
             copy.start()
 
-    for n, known in enumerate((x_line[:2], z_near, z_near, x_line)):
+    for n, known in enumerate(
+        ([x_line[0], z_near[0]], x_line[:2], z_near, z_near, x_line)
+    ):
         for where in known:
             pl.semaphore_signal(met.at[n], inc=1, device_id=where, device_id_type=MESH)
         pl.semaphore_wait(met.at[n], len(known))
@@ -221,10 +226,13 @@
         for j in near + late:
             from_sibling(j, n).wait_recv()
 
+    def rows_of(k):
+        return pl.ds(STARTS[k], CHUNKS[k])
+
     def attend(k, first=False):
         def gather(i, carry):
-            b = order[0, k * CB + i]
-            n = order[1, k * CB + i]
+            b = order[0, STARTS[k] // BLK + i]
+            n = order[1, STARTS[k] // BLK + i]
             at = pl.ds(pl.multiple_of(i * 8, 8), 8)
             qb, ob, mb, lb = qf[b], oown[b], mown[b], lown[b]
             for h in range(LH):
@@ -236,21 +244,22 @@
             vc[at, :] = (lax.broadcasted_iota(jnp.int32, (8, HD), 0) < n).astype(F32)
             return carry
 
-        lax.fori_loop(0, CB, gather, 0)
+        lax.fori_loop(0, CHUNKS[k] // BLK, gather, 0)
 
         if first:
             all_here(1)
-        rows = LH * CR
-        qb = qc[...].reshape(rows, HD).astype(BF16)
+        size = CHUNKS[k]
+        rows = LH * size
+        qb = qc[:, :size].reshape(rows, HD).astype(BF16)
         top = None
         for j in range(8):
             s = lax.dot_general(
                 qb, kv[j, :, 0:128, :].reshape(256, HD), NT, preferred_element_type=F32
             )
-            scores[j] = s
+            scores[j, :rows] = s
             both = jnp.maximum(s[:, :HD], s[:, HD:])
             top = both if top is None else jnp.maximum(top, both)
-        m_own = mc[...].reshape(rows, HD)
+        m_own = mc[:, :size].reshape(rows, HD)
         m = jnp.maximum(jnp.max(top, axis=1, keepdims=True) * SCALE, m_own)
         wide = jnp.concatenate([m, m], axis=1)
         if first:
@@ -258,27 +267,27 @@
         acc = jnp.zeros((rows, HD), F32)
         sums = jnp.zeros((rows, HD), F32)
         for j in range(8):
-            e = jnp.exp2(scores[j] * SCALE - wide)
+            e = jnp.exp2(scores[j, :rows] * SCALE - wide)
             sums = sums + (e[:, :HD] + e[:, HD:])
             acc = acc + jnp.dot(
                 e.astype(BF16), kv[j, :, 128:256, :].reshape(256, HD), preferred_element_type=F32
             )
         a = jnp.exp2(m_own - m)
-        total = jnp.sum(sums, axis=1, keepdims=True) + a * lc[...].reshape(rows, HD)
-        o = (acc + a * oc[...].reshape(rows, HD)) / total
-        good = vc[...] > 0.5
+        total = jnp.sum(sums, axis=1, keepdims=True) + a * lc[:, :size].reshape(rows, HD)
+        o = (acc + a * oc[:, :size].reshape(rows, HD)) / total
+        good = vc[:size] > 0.5
         for h in range(LH):
-            v = jnp.where(good, o[h * CR : (h + 1) * CR], 0.0)
-            ctx[k, c, :, h * HD : (h + 1) * HD] = v.astype(BF16)
+            v = jnp.where(good, o[h * size : (h + 1) * size], 0.0)
+            ctx[c, rows_of(k), h * HD : (h + 1) * HD] = v.astype(BF16)
 
     def ctx_copy(k, core):
-        slot = ctx.at[k, core]
+        slot = ctx.at[core, rows_of(k)]
         return remote(slot, slot, c_send.at[k], c_recv.at[k], (bulk, tp_at(0, 0, oth)))
 
     def project(k, dy, dzh):
         n = lax.rem(zh + dzh, NZH) * NY + lax.rem(y + dy, NY)
-        return jnp.dot(ctx[k, 0], wbuf[0, n], preferred_element_type=F32) + jnp.dot(
-            ctx[k, 1], wbuf[1, n], preferred_element_type=F32
+        return jnp.dot(ctx[0, rows_of(k)], wbuf[0, n], preferred_element_type=F32) + jnp.dot(
+            ctx[1, rows_of(k)], wbuf[1, n], preferred_element_type=F32
         )
 
     up, down = (bulk, tp_at(0, 1, c)), (bulk, tp_at(0, 3, c))
@@ -286,13 +295,13 @@
 
     def d2_copy(k, side):
         return remote(
-            d2s.at[k, side], d2r.at[k, side], d2_send.at[k, side], d2_recv.at[k, side], toward[side]
+            d2s.at[side, rows_of(k)], d2r.at[side, rows_of(k)], d2_send.at[k, side], d2_recv.at[k, side], toward[side]
         )
 
     def b_copy(k, side, dzh):
         return remote(
-            bs.at[k, side, dzh],
-            br.at[k, side, dzh],
+            bs.at[side, dzh, rows_of(k)],
+            br.at[side, dzh, rows_of(k)],
             b_send.at[k, side, dzh],
             b_recv.at[k, side, dzh],
             toward[side],
@@ -301,69 +310,58 @@
     def first_sends(k):
         ctx_copy(k, oth).wait_recv()
         for side in range(2):
-            d2s[k, side] = project(k, 2, side).astype(BF16)
+            d2s[side, rows_of(k)] = project(k, 2, side).astype(BF16)
             d2_copy(k, side).start()
         for side in range(2):
             dzh = 1 - side
-            bs[k, side, dzh] = project(k, 1 + 2 * side, dzh).astype(BF16)
+            bs[side, dzh, rows_of(k)] = project(k, 1 + 2 * side, dzh).astype(BF16)
             b_copy(k, side, dzh).start()
 
     def merged_sends(k):
         for side in range(2):
             mine = project(k, 1 + 2 * side, side)
             d2_copy(k, side).wait_recv()
-            bs[k, side, side] = (mine + d2r[k, side].astype(F32)).astype(BF16)
+            bs[side, side, rows_of(k)] = (mine + d2r[side, rows_of(k)].astype(F32)).astype(BF16)
             b_copy(k, side, side).start()
 
     mine32 = pl.ds(pl.multiple_of(bulk * 32, 32), 32)
 
-    def x_copy(k, n, dzh):
+    def x_copy(p, dzh):
         return remote(
-            ds.at[k, dzh, pl.ds(n * 32, 32), :],
+            ds.at[dzh, pl.ds(p * SEND, SEND), :],
             out.at[dzh, mine32, :],
-            x_send.at[k, n, dzh],
-            x_recv.at[k, n, dzh],
-            (bulk_at(lax.rem(lax.div(k, NK // NX) + 1, NX), lax.rem(k, NK // NX) * DZ + n), tp_at(dzh, 0, c)),
+            x_send.at[p, dzh],
+            x_recv.at[p, dzh],
+            (bulk_at((p // NZL + 1) % NX, p % NZL), tp_at(dzh, 0, c)),
         )
 
     def stay():
-        return pltpu.make_async_copy(ds.at[NK - NK // NX, 0, 0:32, :], out.at[0, mine32, :], q_sem)
-
-    def x_half(k, dzh, do):
-        for n in range(DZ):
-            if n or dzh:
-                do(x_copy(k, n, dzh))
-            else:
-
-                @pl.when(k != NK - NK // NX)
-                def _():
-                    do(x_copy(k, 0, 0))
-
-    def x_each(k, do):
-        for dzh in range(NZH):
-            x_half(k, dzh, do)
+        return pltpu.make_async_copy(ds.at[0, pl.ds(STAYS * SEND, SEND), :], out.at[0, mine32, :], q_sem)
+
+    def x_half(k, dzh):
+        places = range(STARTS[k] // SEND, (STARTS[k] + CHUNKS[k]) // SEND)
+        return [x_copy(p, dzh) for p in places if dzh or p != STAYS]
 
     def finish(k):
         def gather(i, carry):
-            b = order[0, k * CB + i]
-            n = order[1, k * CB + i]
+            b = order[0, STARTS[k] // BLK + i]
+            n = order[1, STARTS[k] // BLK + i]
             row = lax.broadcasted_iota(jnp.int32, (8, FE), 0)
             rc[pl.ds(pl.multiple_of(i * 8, 8), 8), :] = jnp.where(row < n, rf[b], 0.0)
             return carry
 
-        lax.fori_loop(0, CB, gather, 0)
+        lax.fori_loop(0, CHUNKS[k] // BLK, gather, 0)
         for dzh in (1, 0):
             mine = project(k, 0, dzh)
             if dzh == 0:
-                mine = mine + rc[...]
+                mine = mine + rc[: CHUNKS[k]]
             for side in (1 - dzh, dzh):
                 b_copy(k, side, dzh).wait_recv()
-                mine = mine + br[k, side, dzh].astype(F32)
-            ds[k, dzh] = mine.astype(BF16)
-            x_half(k, dzh, lambda copy: copy.start())
-
-        @pl.when(k == NK - NK // NX)
-        def _():
+                mine = mine + br[side, dzh, rows_of(k)].astype(F32)
+            ds[dzh, rows_of(k)] = mine.astype(BF16)
+            for copy in x_half(k, dzh):
+                copy.start()
+        if STARTS[k] <= STAYS * SEND < STARTS[k] + CHUNKS[k]:
             stay().start()
 
     def w_from_sibling(n):
@@ -380,33 +378,21 @@
     ctx_copy(0, c).start()
     lax.fori_loop(0, 8, weights, 0)
 
-    def step(k, carry):
-        @pl.when(k > 0)
-        def _():
+    for k in range(NK + 1):
+        if k > 0:
             merged_sends(k - 1)
-
-        @pl.when(k < NK)
-        def _():
+        if k < NK:
             first_sends(k)
-
-        @pl.when(k < NK - 1)
-        def _():
+        if k < NK - 1:
             attend(k + 1)
             ctx_copy(k + 1, c).start()
-
-        @pl.when(k > 0)
-        def _():
+        if k > 0:
             finish(k - 1)
 
-        return carry
-
-    lax.fori_loop(0, NK + 1, step, 0)
-
-    def collect(k, carry):
-        x_each(k, lambda copy: copy.wait_recv())
-        return carry
-
-    lax.fori_loop(0, NK, collect, 0)
+    for k in range(NK):
+        for dzh in range(NZH):
+            for copy in x_half(k, dzh):
+                copy.wait_recv()
     stay().wait()
 
     for j in range(1, 8):
@@ -421,16 +407,15 @@
 
     lax.fori_loop(0, 8, left, 0)
 
-    def left_k(k, carry):
+    for k in range(NK):
         ctx_copy(k, c).wait_send()
         for side in range(2):
             d2_copy(k, side).wait_send()
             for dzh in range(NZH):
                 b_copy(k, side, dzh).wait_send()
-        x_each(k, lambda copy: copy.wait_send())
-        return carry
-
-    lax.fori_loop(0, NK, left_k, 0)
+        for dzh in range(NZH):
+            for copy in x_half(k, dzh):
+                copy.wait_send()
 
 
 def local(queries, comp_keys, comp_values, prefix_keys, prefix_values, lengths, routing, residual, out_weight):
@@ -460,20 +445,20 @@
             vmem((LH, CR, HD), F32),
             vmem((CR, HD), F32),
             vmem((CR, FE), F32),
-            vmem((NK, 2, CR, FE), BF16),
-            vmem((NK, 2, CR, FE), BF16),
-            vmem((NK, 2, CR, FE), BF16),
-            vmem((NK, 2, 2, CR, FE), BF16),
-            vmem((NK, 2, 2, CR, FE), BF16),
-            vmem((NK, 2, CR, FE), BF16),
+            vmem((2, 512, FE), BF16),
+            vmem((2, 512, FE), BF16),
+            vmem((2, 512, FE), BF16),
+            vmem((2, 2, 512, FE), BF16),
+            vmem((2, 2, 512, FE), BF16),
+            vmem((2, 512, FE), BF16),
             vmem((8, 128), jnp.int32),
             pltpu.SMEM((8, 128), jnp.int32),
-            pltpu.SemaphoreType.REGULAR((4,)),
+            pltpu.SemaphoreType.REGULAR((5,)),
             dma,
             dma, dma, dma((4,)), dma((8, 4)), dma((8, 4)), dma((8, 3)), dma((8, 3)),
             dma((8,)), dma((8,)), dma((8,)),
             dma((NK,)), dma((NK,)), dma((NK, 2)), dma((NK, 2)), dma((NK, 2, 2)), dma((NK, 2, 2)),
-            dma((NK, DZ, 2)), dma((NK, DZ, 2)),
+            dma((ND, 2)), dma((ND, 2)),
         ],
         compiler_params=pltpu.CompilerParams(
             collective_id=0, has_side_effects=True, vmem_limit_bytes=56 * 2**20

time: 81 us -> 80.1 us (0.989)
  no operation moved by 1% of the time
where the time goes in v4:
time: 80.1 us; the launch traced here: 79.6 us
  Pallas kernels  78.6 us (98%)
  other arithmetic  0.93 us (1%)
    pallas_call x1, Pallas kernels, local(): pl.pallas_call(main_kernel, out_shape=pltpu.VMEM((NZH, 512, FE), BF16), i...  78.6 us

profile of v4, /device:TPU:2, one launch (start us, length us, event | category | flops | bytes accessed | tf_op | source)
XLA Modules:
  0.0 79.6 jit_solution(3480285203937118599)
XLA Ops:
  0.0 78.6 %attend_project_send.1 = bf16[2,512,512]{2,1,0:T(8,128)(2,1)S(1)} custom-call(s32[1,16]{1,0:T(1,128)} %lens.1, s32[1,64]{1,0:T(1,128)} %route.1, bf16[1024,512]{1,0:T(8,128)(2,1)} %q.1, bf16[64,1024]{1,0:T(8,128)(2,1)} %ck.1, bf16[64,1024]{1,0:T(8,128)(2,1)} %cv.1, bf16[1,128,1024]{2,1,0:T(8,128)(2,1)} %pk.1, bf16[1,128,1024]{2,1,0:T(8,128)(2,1)} %pv.1, ...), custom_call_target="tpu_custom_call" | custom-call | tf_op jit(solution)/shard_map/attend_project_send/pallas_call | solution.py:426
  78.6 0.9 %fusion = bf16[512,512]{1,0:T(8,128)(2,1)} fusion(bf16[2,512,512]{2,1,0:T(8,128)(2,1)S(1)} %attend_project_send.1), kind=kLoop, calls=%fused_computation.1 | loop fusion | flops 1048576 | bytes 1572864 | tf_op jit(solution)/shard_map/convert_element_type | solution.py:468

commit v5 on v4

--- a/solution.py
+++ b/solution.py
@@ -142,10 +142,6 @@
         )
         return here, away
 
-    for n in range(8):
-        for copy in w_copies(n):
-            copy.start()
-
     for n, known in enumerate(
         ([x_line[0], z_near[0]], x_line[:2], z_near, z_near, x_line)
     ):
@@ -158,6 +154,9 @@
     tab[1:2, :] = nval
     t_copy = pltpu.make_async_copy(tab, order, t_sem)
     t_copy.start()
+    for n in range(8):
+        for copy in w_copies(n):
+            copy.start()
     q_copy.wait()
     r_copy.wait()
     t_copy.wait()
@@ -340,7 +339,7 @@
 
     def x_half(k, dzh):
         places = range(STARTS[k] // SEND, (STARTS[k] + CHUNKS[k]) // SEND)
-        return [x_copy(p, dzh) for p in places if dzh or p != STAYS]
+        return [x_copy(p, dzh) for p in (places if dzh else places[::-1]) if dzh or p != STAYS]
 
     def finish(k):
         def gather(i, carry):

time: 80.1 us -> 80.1 us (level)
  no operation moved by 1% of the time
where the time goes in v5:
time: 80.1 us; the launch traced here: 80 us
  Pallas kernels  79.1 us (99%)
  other arithmetic  0.93 us (1%)
    pallas_call x1, Pallas kernels, local(): pl.pallas_call(main_kernel, out_shape=pltpu.VMEM((NZH, 512, FE), BF16), i...  79.1 us

profile of v5, /device:TPU:2, one launch (start us, length us, event | category | flops | bytes accessed | tf_op | source)
XLA Modules:
  0.0 80.0 jit_solution(5099363007929092563)
XLA Ops:
  0.0 79.1 %attend_project_send.1 = bf16[2,512,512]{2,1,0:T(8,128)(2,1)S(1)} custom-call(s32[1,16]{1,0:T(1,128)} %lens.1, s32[1,64]{1,0:T(1,128)} %route.1, bf16[1024,512]{1,0:T(8,128)(2,1)} %q.1, bf16[64,1024]{1,0:T(8,128)(2,1)} %ck.1, bf16[64,1024]{1,0:T(8,128)(2,1)} %cv.1, bf16[1,128,1024]{2,1,0:T(8,128)(2,1)} %pk.1, bf16[1,128,1024]{2,1,0:T(8,128)(2,1)} %pv.1, ...), custom_call_target="tpu_custom_call" | custom-call | tf_op jit(solution)/shard_map/attend_project_send/pallas_call | solution.py:425
  79.1 0.9 %fusion = bf16[512,512]{1,0:T(8,128)(2,1)} fusion(bf16[2,512,512]{2,1,0:T(8,128)(2,1)S(1)} %attend_project_send.1), kind=kLoop, calls=%fused_computation.1 | loop fusion | flops 1048576 | bytes 1572864 | tf_op jit(solution)/shard_map/convert_element_type | solution.py:467
